TPU v7x, 32 devices: a whole 2x2x4 slice. The times are simulated.
32 devices in a mesh: row: 8 (over z, core), col: 4 (over y, x).
Axes of the slice: x: 2, y: 2, z: 4, core: 2. Of those that a mesh axis runs over, the one named last changes fastest.
Arguments:
- amplitudes: bfloat16 [256, 4, 16384], P('col', None, 'row'), may hold values from -6 to 6
- integrals: bfloat16 [4, 16384, 16384], P(None, 'row', 'col'), may hold values from -0.046875 to 0.046875
- block_sizes: int32 [4], replicated, may hold values from 8192 to 16384, as said below
Outputs:
- ladder: float32 [256, 4, 16384], P('row', None, 'col')
Inputs may be any that keep to these rules, and one draw needn't show every extreme that they name: Each irrep block uses its first block_sizes[h] pairs; in every draw some block uses all 16384.
All inputs are finite; a program needn't handle non-finite values.
Results may differ from a plain program's by a relative error of at most 0.0003.
Values may be sent and summed in bfloat16 or wider, within the bound.
A program may use at most 128 MiB of HBM per device.

v0:
```python
import jax
import jax.numpy as jnp
from jax import lax
from jax.sharding import PartitionSpec as P


def body(amplitudes, integrals, block_sizes):
    nblocks, span, width = integrals.shape
    row_low = lax.axis_index("row") * span
    col_low = lax.axis_index("col") * width
    k_index = row_low + lax.iota(jnp.int32, span)
    q_index = col_low + lax.iota(jnp.int32, width)
    live_k = k_index[None, :] < block_sizes[:, None]
    live_q = q_index[None, :] < block_sizes[:, None]
    masked = jnp.where(live_k[None], amplitudes, jnp.zeros((), amplitudes.dtype))
    partial_value = jnp.einsum(
        "pha,hab->phb",
        lax.all_gather(masked, "col", axis=0, tiled=True),
        integrals,
        preferred_element_type=jnp.float32,
    )
    summed = lax.psum_scatter(partial_value, "row", scatter_dimension=0, tiled=True)
    return jnp.where(live_q[None], summed, jnp.zeros((), jnp.float32))


def solution(mesh):
    placed = (P("col", None, "row"), P(None, "row", "col"), P())
    return jax.shard_map(
        body, mesh=mesh, in_specs=placed, out_specs=P("row", None, "col"), check_vma=False
    )
```

profile of v0, /device:TPU:0, one launch (start us, length us, event | category | flops | bytes accessed | tf_op | source)
XLA Modules:
  0.0 277.7 jit_solution(1234716045798428063)
XLA Ops:
  6.5 0.0 all-gather.2.cloned.1.call-start
  6.5 0.7 broadcast_compare_fusion.1
  7.3 3.4 %copy_select_fusion = bf16[64,4,2048]{2,0,1:T(8,128)(2,1)} fusion(bf16[64,4,2048]{2,1,0:T(4,128)(2,1)} %param.3, pred[4,2048]{1,0:T(4,128)(4,1)S(1)} %broadcast_compare_fusion.1), kind=kLoop, calls=%fused_computation.1 | loop fusion | flops 524288 | bytes 2105344 | tf_op jit(solution)/shard_map/jit(_where)/select_n | solution.py:15
  10.7 0.0 all-gather.2.cloned.1.call-update
  10.7 0.0 reduce-scatter.2.cloned.1.call-start
  10.8 55.4 %all-gather.2.cloned.1.call-done = bf16[256,4,2048]{2,0,1:T(8,128)(2,1)} async-done(((bf16[64,4,2048]{2,0,1:T(8,128)(2,1)}), bf16[256,4,2048]{2,0,1:T(8,128)(2,1)}) %all-gather.2.cloned.1.call-update) | async-done | bytes 4194320 | tf_op jit(solution)/shard_map/all_gather | solution.py:18
  66.2 31.9 %convolution_bitcast_fusion = f32[256,4,4096]{2,0,1:T(8,128)} fusion(bf16[256,4,2048]{2,0,1:T(8,128)(2,1)} %all-gather.2.cloned.1.call-done, bf16[4,2048,4096]{2,1,0:T(8,128)(2,1)} %param.4), kind=kOutput, calls=%fused_computation | convolution fusion | flops 17179869184 | bytes 88080384 | tf_op jit(solution)/shard_map/pha,hab->phb/dot_general | solution.py:16
  98.0 0.0 copy-start
  98.0 0.0 reduce-scatter.2.cloned.1.call-update
  98.1 0.6 copy-done
  98.7 0.1 broadcast_compare_fusion
  98.8 167.6 %reduce-scatter.2.cloned.1.call-done = f32[32,4,4096]{2,0,1:T(8,128)} async-done(((f32[256,4,4096]{2,0,1:T(8,128)}), f32[32,4,4096]{2,0,1:T(8,128)}) %reduce-scatter.2.cloned.1.call-update) | async-done | bytes 2097168 | tf_op jit(solution)/shard_map/reduce_scatter | solution.py:22
  266.4 1.8 broadcast_select_fusion
  268.2 2.7 copy.5
  (2 shorter events, 0.0 us)
Async XLA Ops:
  6.5 59.6 %all-gather.2.cloned.1.call-start = ((), (), s32[]{:S(2)}) async-start(), calls=%async_computation.1 | async-start | bytes 5242880 | tf_op jit(solution)/shard_map/all_gather | solution.py:18
  10.7 255.6 %reduce-scatter.2.cloned.1.call-start = ((), (), s32[]{:S(2)}) async-start(), calls=%async_computation.2 | async-start | bytes 18874368 | tf_op jit(solution)/shard_map/reduce_scatter | solution.py:22
  98.0 0.7 copy-start
Sparse Core Ops, SparseCore 0:
  10.8 55.2 all-gather.1
  98.2 168.1 reduce-scatter.1
where the time goes:
time: 278 us
  waiting for transfers between devices  223 us (80%)
  matrix products  31.9 us (11%)
  between operations  13.4 us (5%)
  other arithmetic  6.1 us (2%)
  local copies, waits for them, and re-layouts  3.28 us (1%)
    reduce_scatter x1, waiting for transfers between devices, body(): lax.psum_scatter(partial_value, 'row', scatter_dimension=0, tiled=True)  168 us
    all_gather x1, waiting for transfers between devices, body(): lax.all_gather(masked, 'col', axis=0, tiled=True)  55.4 us
    dot_general x1, matrix products, body(): jnp.einsum('pha,hab->phb', lax.all_gather(masked, 'col', axis=0, tiled=Tr...  31.9 us
  transfers between devices with their start and end apart: 2, of which 2 were waited for; matrix products, arithmetic and copies ran while one was open for 0% of the time, Pallas kernels for 0%

commit v1 on v0

v1 whole, which is shorter than its diff:
```python
import functools

import jax
import jax.numpy as jnp
from jax import lax
from jax.experimental import pallas as pl
from jax.experimental.pallas import tpu as pltpu
from jax.sharding import PartitionSpec as P

CORES = 2
SLOTS = 3
TILE = 256
LAG = 2
TOP = 32766.0
TINY = 1e-30


def kernel(chips, cols, steps, chunk, sizes, amp, integ, out, gathered, masked, panel, part, peer, stage, inbox,
           scale_out, scale_in, own_sem, gather_send, gather_recv, panel_sem, peer_send, peer_recv,
           stage_send, inbox_recv, scale_send, scale_recv):
    row, col = lax.axis_index("row"), lax.axis_index("col")
    z, core = row // CORES, row % CORES
    blocks, share, span = amp.shape
    pairs = stage.shape[2]
    per_block = steps // blocks
    width = chunk * per_block
    mate = z * CORES + 1 - core

    def send(src, dst, send_sem, recv_sem, to_row, to_col):
        return pltpu.make_async_remote_copy(
            src_ref=src, dst_ref=dst, send_sem=send_sem, recv_sem=recv_sem,
            device_id={"row": to_row, "col": to_col}, device_id_type=pl.DeviceIdType.MESH)

    def panel_copy(t):
        lanes = pl.ds(pl.multiple_of((t % per_block) * chunk, chunk), chunk)
        slot = t % SLOTS
        return pltpu.make_async_copy(integ.at[t // per_block, :, lanes], panel.at[slot], panel_sem.at[slot])

    def gather_copy(h, k):
        return send(amp.at[h], gathered.at[h, col], gather_send.at[h, k], gather_recv.at[h, col],
                    row, (col + k) % cols)

    def gather_wait(h, k):
        source = (col + k) % cols
        send(amp.at[h], gathered.at[h, source], gather_send.at[h, k], gather_recv.at[h, source], row, source).wait_recv()

    def own_copy(h):
        return pltpu.make_async_copy(amp.at[h], gathered.at[h, col], own_sem.at[h])

    def peer_copy(t):
        return send(part.at[t, :, 1 - core], peer.at[t], peer_send.at[t], peer_recv.at[t], mate, col)

    def data_copy(t, d, way, to_row):
        slot = d + 1 - way
        return send(stage.at[t, d], inbox.at[t, slot], stage_send.at[t, d], inbox_recv.at[t, slot], to_row, col)

    def scale_copy(t, way, to_row):
        return send(scale_out.at[way, t], scale_in.at[way, t], scale_send.at[way, t], scale_recv.at[way, t], to_row, col)

    def loop(low, high, body):
        lax.fori_loop(low, high, lambda i, c: (body(i), c)[1], 0)

    for t in range(min(SLOTS, steps)):
        panel_copy(t).start()
    loop(0, blocks, lambda h: own_copy(h).start())

    barrier = pltpu.get_barrier_semaphore()

    def greet(to_row, to_col):
        pl.semaphore_signal(barrier, inc=1, device_id={"row": to_row, "col": to_col},
                            device_id_type=pl.DeviceIdType.MESH)

    loop(1, cols, lambda k: greet(row, (col + k) % cols))
    greet(mate, col)

    @pl.when(z > 0)
    def _():
        greet(row - CORES, col)

    @pl.when(z < chips - 1)
    def _():
        greet(row + CORES, col)

    pl.semaphore_wait(barrier, cols + jnp.where(z > 0, 1, 0) + jnp.where(z < chips - 1, 1, 0))

    loop(0, blocks, lambda h: loop(1, cols, lambda k: gather_copy(h, k).start()))

    def compute(t):
        h = t // per_block

        @pl.when(t % per_block == 0)
        def _():
            own_copy(h).wait()
            loop(1, cols, lambda k: gather_wait(h, k))
            index = row * span + lax.broadcasted_iota(jnp.int32, (share, span), 1)
            live = index < sizes[h]

            def fill(c):
                values = jnp.where(live, gathered[h, c].astype(jnp.float32), 0.0)
                masked[pl.ds(pl.multiple_of(c * share, share), share), :] = values.astype(masked.dtype)

            loop(0, cols, fill)

        panel_copy(t).wait()
        slot = t % SLOTS

        def tile(n):
            lanes = pl.ds(pl.multiple_of(n * TILE, TILE), TILE)
            value = jnp.dot(masked[...], panel[slot, :, lanes], preferred_element_type=jnp.float32)
            part[t, :, :, :, lanes] = value.reshape(chips, CORES, pairs, TILE)

        loop(0, chunk // TILE, tile)
        peer_copy(t).start()

        @pl.when(t + SLOTS < steps)
        def _():
            panel_copy(t + SLOTS).start()

    def combine(t):
        peer_copy(t).wait_recv()

        def add(d):
            part[t, d, core] = part[t, d, core] + peer[t, d]

        loop(0, chips, add)

    def relay(t, way):
        up = way == 0
        has_source = z > 0 if up else z < chips - 1
        has_target = z < chips - 1 if up else z > 0
        to_row = row + CORES if up else row - CORES
        first, last = (z + 1, chips) if up else (0, z)

        @pl.when(has_source)
        def _():
            scale_copy(t, way, row).wait_recv()
            factor = scale_in[way, t]

            def take(d):
                data_copy(t, d, way, row).wait_recv()
                part[t, d, core] = part[t, d, core] + inbox[t, d + 1 - way].astype(jnp.int32).astype(jnp.float32) * factor

            loop(*((z, chips) if up else (0, z + 1)), take)

        @pl.when(has_target)
        def _():
            largest = lax.fori_loop(
                first, last,
                lambda d, m: jnp.maximum(m, jnp.max(jnp.abs(part[t, d, core]), axis=0, keepdims=True)),
                jnp.full((1, chunk), TINY, jnp.float32))
            scale_out[way, t] = largest * (1.0 / TOP)
            scale_copy(t, way, to_row).start()
            inverse = TOP / largest

            def put(d):
                stage[t, d] = jnp.round(part[t, d, core] * inverse).astype(jnp.int32).astype(jnp.int16)
                data_copy(t, d, way, to_row).start()

            loop(0, last - first, (lambda j: put(last - 1 - j)) if up else put)

    def finish(t):
        h = t // per_block
        low = (t % per_block) * chunk
        index = col * width + low + lax.broadcasted_iota(jnp.int32, (pairs, chunk), 1)
        out[h, :, pl.ds(pl.multiple_of(low, chunk), chunk)] = jnp.where(index < sizes[h], part[t, z, core], 0.0)

    def at(t, body):
        @pl.when(jnp.logical_and(t >= 0, t < steps))
        def _():
            body(t)

    up_lag = 1 + LAG * z
    down_lag = 1 + LAG * (chips - 1 - z)
    end_lag = 1 + LAG * chips

    def step(i):
        at(i, compute)
        at(i - 1, combine)
        at(i - up_lag, lambda t: relay(t, 0))
        at(i - down_lag, lambda t: relay(t, 1))
        at(i - end_lag, finish)

    loop(0, steps + end_lag, step)

    loop(0, blocks, lambda h: loop(1, cols, lambda k: gather_copy(h, k).wait_send()))

    def drain(t):
        peer_copy(t).wait_send()

        @pl.when(z < chips - 1)
        def _():
            scale_copy(t, 0, row).wait_send()
            loop(z + 1, chips, lambda d: data_copy(t, d, 0, row).wait_send())

        @pl.when(z > 0)
        def _():
            scale_copy(t, 1, row).wait_send()
            loop(0, z, lambda d: data_copy(t, d, 1, row).wait_send())

    loop(0, steps, drain)


def body(chips, cols, amplitudes, integrals, block_sizes):
    share, blocks, span = amplitudes.shape
    width = integrals.shape[2]
    chunk = min(1024, width)
    steps = blocks * (width // chunk)
    total = share * cols
    pairs = total // (chips * CORES)
    dma = pltpu.SemaphoreType.DMA
    result = pl.pallas_call(
        functools.partial(kernel, chips, cols, steps, chunk),
        out_shape=jax.ShapeDtypeStruct((blocks, pairs, width), jnp.float32),
        in_specs=[
            pl.BlockSpec(memory_space=pltpu.SMEM),
            pl.BlockSpec(memory_space=pl.ANY),
            pl.BlockSpec(memory_space=pl.ANY),
        ],
        out_specs=pl.BlockSpec(memory_space=pltpu.VMEM),
        scratch_shapes=[
            pltpu.VMEM((blocks, cols, share, span), amplitudes.dtype),
            pltpu.VMEM((total, span), amplitudes.dtype),
            pltpu.VMEM((SLOTS, span, chunk), integrals.dtype),
            pltpu.VMEM((steps, chips, CORES, pairs, chunk), jnp.float32),
            pltpu.VMEM((steps, chips, pairs, chunk), jnp.float32),
            pltpu.VMEM((steps, chips, pairs, chunk), jnp.int16),
            pltpu.VMEM((steps, chips + 1, pairs, chunk), jnp.int16),
            pltpu.VMEM((2, steps, 1, chunk), jnp.float32),
            pltpu.VMEM((2, steps, 1, chunk), jnp.float32),
            dma((blocks,)),
            dma((blocks, cols)),
            dma((blocks, cols)),
            dma((SLOTS,)),
            dma((steps,)),
            dma((steps,)),
            dma((steps, chips)),
            dma((steps, chips + 1)),
            dma((2, steps)),
            dma((2, steps)),
        ],
        compiler_params=pltpu.CompilerParams(
            collective_id=0, has_side_effects=True, vmem_limit_bytes=63 * 2**20
        ),
        name="ladder",
    )(block_sizes, amplitudes.transpose(1, 0, 2), integrals)
    return result.transpose(1, 0, 2)


def solution(mesh):
    placed = (P("col", None, "row"), P(None, "row", "col"), P())
    return jax.shard_map(
        functools.partial(body, mesh.shape["row"] // CORES, mesh.shape["col"]),
        mesh=mesh, in_specs=placed, out_specs=P("row", None, "col"), check_vma=False,
    )
```

time: 278 us -> 114 us (0.41)
  waiting for transfers between devices: 223 us -> 0 us
  Pallas kernels: 0 us -> 107 us
  matrix products: 31.9 us -> 0 us
  between operations: 13.4 us -> 0.01 us
  other arithmetic: 6.1 us -> 0 us
  local copies, waits for them, and re-layouts: 3.28 us -> 7.03 us
    reduce_scatter x1 -> x0, waiting for transfers between devices: 168 us -> none  [body(): lax.psum_scatter(partial_value, 'row', scatter_dimension=0, tiled=True)]
    pallas_call x0 -> x1, Pallas kernels: none -> 107 us  [body(): pl.pallas_call(functools.partial(kernel, chips, cols, steps, chunk), out_...]
    all_gather x1 -> x0, waiting for transfers between devices: 55.4 us -> none  [body(): lax.all_gather(masked, 'col', axis=0, tiled=True)]
    dot_general x1 -> x0, matrix products: 31.9 us -> none  [body(): jnp.einsum('pha,hab->phb', lax.all_gather(masked, 'col', axis=0, tiled=Tr...]
    select_n x2 -> x0, other arithmetic: 5.26 us -> none  [the longest x1 3.43 us: body(): jnp.where(live_k[None], amplitudes, jnp.zeros((), amplitudes.dtype))]
    transpose x0 -> x1, local copies, waits for them, and re-layouts: none -> 4.26 us  [body(): return result.transpose(1, 0, 2)]
  transfers between devices with their start and end apart: 2 -> 0, of which waited for: 2 -> 0; matrix products, arithmetic and copies ran while one was open for 0% -> 0% of each run, Pallas kernels for 0% -> 0%
where the time goes in v1:
time: 114 us
  Pallas kernels  107 us (94%)
  local copies, waits for them, and re-layouts  7.03 us (6%)
    pallas_call x1, Pallas kernels, body(): pl.pallas_call(functools.partial(kernel, chips, cols, steps, chunk), out_...  107 us
    transpose x1, local copies, waits for them, and re-layouts, body(): return result.transpose(1, 0, 2)  4.26 us
    unnamed x1, local copies, waits for them, and re-layouts  2.77 us

profile of v1, /device:TPU:0, one launch (start us, length us, event | category | flops | bytes accessed | tf_op | source)
XLA Modules:
  0.0 114.0 jit_solution(8696376006680545372)
XLA Ops:
  0.0 2.8 %copy.7 = bf16[64,4,2048]{2,0,1:T(8,128)(2,1)} copy(bf16[64,4,2048]{2,1,0:T(4,128)(2,1)} %param.3) | data formatting | bytes 2097152 | tf_op args[0]
  2.8 107.0 %ladder.1 = f32[4,32,4096]{2,1,0:T(8,128)} custom-call(s32[4]{0:T(128)} %sizes.1, bf16[4,64,2048]{2,1,0:T(8,128)(2,1)} %bitcast.5, bf16[4,2048,4096]{2,1,0:T(8,128)(2,1)} %integ.1), custom_call_target="tpu_custom_call" | custom-call | tf_op jit(solution)/shard_map/ladder/pallas_call | solution.py:211
  109.7 4.3 %copy.5 = f32[32,4,4096]{2,1,0:T(4,128)} copy(f32[32,4,4096]{2,0,1:T(8,128)} %bitcast.4) | data formatting | bytes 4194304 | tf_op jit(solution)/shard_map/transpose | solution.py:246

commit v2 on v1

--- a/solution.py
+++ b/solution.py
@@ -8,7 +8,7 @@
 from jax.sharding import PartitionSpec as P
 
 CORES = 2
-SLOTS = 3
+SLOTS = 4
 TILE = 256
 LAG = 2
 TOP = 32766.0
@@ -20,9 +20,9 @@
            stage_send, inbox_recv, scale_send, scale_recv):
     row, col = lax.axis_index("row"), lax.axis_index("col")
     z, core = row // CORES, row % CORES
-    blocks, share, span = amp.shape
-    pairs = stage.shape[2]
+    blocks, _, pairs, span = amp.shape
     per_block = steps // blocks
+    early = min(per_block, SLOTS)
     width = chunk * per_block
     mate = z * CORES + 1 - core
 
@@ -36,19 +36,20 @@
         slot = t % SLOTS
         return pltpu.make_async_copy(integ.at[t // per_block, :, lanes], panel.at[slot], panel_sem.at[slot])
 
-    def gather_copy(h, k):
-        return send(amp.at[h], gathered.at[h, col], gather_send.at[h, k], gather_recv.at[h, col],
+    def gather_copy(h, q, k):
+        return send(amp.at[h, q], gathered.at[h, q, col], gather_send.at[h, q, k], gather_recv.at[h, q, col],
                     row, (col + k) % cols)
 
-    def gather_wait(h, k):
+    def gather_wait(h, q, k):
         source = (col + k) % cols
-        send(amp.at[h], gathered.at[h, source], gather_send.at[h, k], gather_recv.at[h, source], row, source).wait_recv()
-
-    def own_copy(h):
-        return pltpu.make_async_copy(amp.at[h], gathered.at[h, col], own_sem.at[h])
+        send(amp.at[h, q], gathered.at[h, q, source], gather_send.at[h, q, k], gather_recv.at[h, q, source],
+             row, source).wait_recv()
+
+    def own_copy(h, q):
+        return pltpu.make_async_copy(amp.at[h, q], gathered.at[h, q, col], own_sem.at[h, q])
 
     def peer_copy(t):
-        return send(part.at[t, :, 1 - core], peer.at[t], peer_send.at[t], peer_recv.at[t], mate, col)
+        return send(part.at[t, 1 - core], peer.at[t], peer_send.at[t], peer_recv.at[t], mate, col)
 
     def data_copy(t, d, way, to_row):
         slot = d + 1 - way
@@ -62,7 +63,7 @@
 
     for t in range(min(SLOTS, steps)):
         panel_copy(t).start()
-    loop(0, blocks, lambda h: own_copy(h).start())
+    loop(0, blocks, lambda h: loop(0, CORES, lambda q: own_copy(h, q).start()))
 
     barrier = pltpu.get_barrier_semaphore()
 
@@ -83,44 +84,74 @@
 
     pl.semaphore_wait(barrier, cols + jnp.where(z > 0, 1, 0) + jnp.where(z < chips - 1, 1, 0))
 
-    loop(0, blocks, lambda h: loop(1, cols, lambda k: gather_copy(h, k).start()))
-
-    def compute(t):
-        h = t // per_block
-
+    loop(0, blocks, lambda h: loop(0, CORES, lambda q: loop(1, cols, lambda k: gather_copy(h, q, k).start())))
+
+    def prepare(h, q):
+        own_copy(h, q).wait()
+        loop(1, cols, lambda k: gather_wait(h, q, k))
+        index = row * span + lax.broadcasted_iota(jnp.int32, (pairs, span), 1)
+        live = index < sizes[h]
+
+        def fill(c):
+            values = jnp.where(live, gathered[h, q, c].astype(jnp.float32), 0.0)
+            masked[q, pl.ds(pl.multiple_of(c * pairs, pairs), pairs), :] = values.astype(masked.dtype)
+
+        loop(0, cols, fill)
+
+    def next_panel(t):
+        @pl.when(t + SLOTS < steps)
+        def _():
+            panel_copy(t + SLOTS).start()
+
+    def half(t, q):
+        @pl.when(t == 0)
+        def _():
+            prepare(0, q)
+
+        @pl.when(q == 0)
+        def _():
+            panel_copy(t).wait()
+
+        slot = t % SLOTS
+
+        def tile(n):
+            lanes = pl.ds(pl.multiple_of(n * TILE, TILE), TILE)
+            value = jnp.dot(masked[q], panel[slot, :, lanes], preferred_element_type=jnp.float32)
+            part[t, q, :, :, lanes] = value.reshape(chips, pairs, TILE)
+
+        loop(0, chunk // TILE, tile)
+
+        @pl.when(core != q)
+        def _():
+            peer_copy(t).start()
+
+        @pl.when(q == 1)
+        def _():
+            next_panel(t)
+
+    def full(t):
         @pl.when(t % per_block == 0)
         def _():
-            own_copy(h).wait()
-            loop(1, cols, lambda k: gather_wait(h, k))
-            index = row * span + lax.broadcasted_iota(jnp.int32, (share, span), 1)
-            live = index < sizes[h]
-
-            def fill(c):
-                values = jnp.where(live, gathered[h, c].astype(jnp.float32), 0.0)
-                masked[pl.ds(pl.multiple_of(c * share, share), share), :] = values.astype(masked.dtype)
-
-            loop(0, cols, fill)
+            loop(0, CORES, lambda q: prepare(t // per_block, q))
 
         panel_copy(t).wait()
         slot = t % SLOTS
 
         def tile(n):
             lanes = pl.ds(pl.multiple_of(n * TILE, TILE), TILE)
-            value = jnp.dot(masked[...], panel[slot, :, lanes], preferred_element_type=jnp.float32)
-            part[t, :, :, :, lanes] = value.reshape(chips, CORES, pairs, TILE)
+            left = masked[...].reshape(CORES * chips * pairs, span)
+            value = jnp.dot(left, panel[slot, :, lanes], preferred_element_type=jnp.float32)
+            part[t, :, :, :, lanes] = value.reshape(CORES, chips, pairs, TILE)
 
         loop(0, chunk // TILE, tile)
         peer_copy(t).start()
-
-        @pl.when(t + SLOTS < steps)
-        def _():
-            panel_copy(t + SLOTS).start()
+        next_panel(t)
 
     def combine(t):
         peer_copy(t).wait_recv()
 
         def add(d):
-            part[t, d, core] = part[t, d, core] + peer[t, d]
+            part[t, core, d] = part[t, core, d] + peer[t, d]
 
         loop(0, chips, add)
 
@@ -138,7 +169,7 @@
 
             def take(d):
                 data_copy(t, d, way, row).wait_recv()
-                part[t, d, core] = part[t, d, core] + inbox[t, d + 1 - way].astype(jnp.int32).astype(jnp.float32) * factor
+                part[t, core, d] = part[t, core, d] + inbox[t, d + 1 - way].astype(jnp.int32).astype(jnp.float32) * factor
 
             loop(*((z, chips) if up else (0, z + 1)), take)
 
@@ -146,14 +177,14 @@
         def _():
             largest = lax.fori_loop(
                 first, last,
-                lambda d, m: jnp.maximum(m, jnp.max(jnp.abs(part[t, d, core]), axis=0, keepdims=True)),
+                lambda d, m: jnp.maximum(m, jnp.max(jnp.abs(part[t, core, d]), axis=0, keepdims=True)),
                 jnp.full((1, chunk), TINY, jnp.float32))
             scale_out[way, t] = largest * (1.0 / TOP)
             scale_copy(t, way, to_row).start()
             inverse = TOP / largest
 
             def put(d):
-                stage[t, d] = jnp.round(part[t, d, core] * inverse).astype(jnp.int32).astype(jnp.int16)
+                stage[t, d] = jnp.round(part[t, core, d] * inverse).astype(jnp.int32).astype(jnp.int16)
                 data_copy(t, d, way, to_row).start()
 
             loop(0, last - first, (lambda j: put(last - 1 - j)) if up else put)
@@ -162,27 +193,34 @@
         h = t // per_block
         low = (t % per_block) * chunk
         index = col * width + low + lax.broadcasted_iota(jnp.int32, (pairs, chunk), 1)
-        out[h, :, pl.ds(pl.multiple_of(low, chunk), chunk)] = jnp.where(index < sizes[h], part[t, z, core], 0.0)
-
-    def at(t, body):
-        @pl.when(jnp.logical_and(t >= 0, t < steps))
-        def _():
-            body(t)
+        out[h, :, pl.ds(pl.multiple_of(low, chunk), chunk)] = jnp.where(index < sizes[h], part[t, core, z], 0.0)
+
+    def when(condition, body, *args):
+        @pl.when(condition)
+        def _():
+            body(*args)
+
+    def at(j, body):
+        ahead = jnp.logical_and(core == 0, j < early)
+        t = jnp.where(ahead, j, jnp.where(jnp.logical_and(core == 0, j < 2 * early), -1, j - early))
+        when(jnp.logical_and(t >= 0, t < steps), body, t)
 
     up_lag = 1 + LAG * z
     down_lag = 1 + LAG * (chips - 1 - z)
     end_lag = 1 + LAG * chips
 
     def step(i):
-        at(i, compute)
+        when(jnp.logical_and(i < 2 * early, i != early), lambda: half(i % early, i // early))
+        when(jnp.logical_and(i >= 2 * early, i < steps + early), lambda: full(i - early))
         at(i - 1, combine)
         at(i - up_lag, lambda t: relay(t, 0))
         at(i - down_lag, lambda t: relay(t, 1))
         at(i - end_lag, finish)
-
-    loop(0, steps + end_lag, step)
-
-    loop(0, blocks, lambda h: loop(1, cols, lambda k: gather_copy(h, k).wait_send()))
+        when(i == early, lambda: half(0, 1))
+
+    loop(0, steps + early + end_lag, step)
+
+    loop(0, blocks, lambda h: loop(0, CORES, lambda q: loop(1, cols, lambda k: gather_copy(h, q, k).wait_send())))
 
     def drain(t):
         peer_copy(t).wait_send()
@@ -207,6 +245,7 @@
     steps = blocks * (width // chunk)
     total = share * cols
     pairs = total // (chips * CORES)
+    assert share == CORES * pairs and chips == cols
     dma = pltpu.SemaphoreType.DMA
     result = pl.pallas_call(
         functools.partial(kernel, chips, cols, steps, chunk),
@@ -218,18 +257,18 @@
         ],
         out_specs=pl.BlockSpec(memory_space=pltpu.VMEM),
         scratch_shapes=[
-            pltpu.VMEM((blocks, cols, share, span), amplitudes.dtype),
-            pltpu.VMEM((total, span), amplitudes.dtype),
+            pltpu.VMEM((blocks, CORES, cols, pairs, span), amplitudes.dtype),
+            pltpu.VMEM((CORES, chips * pairs, span), amplitudes.dtype),
             pltpu.VMEM((SLOTS, span, chunk), integrals.dtype),
-            pltpu.VMEM((steps, chips, CORES, pairs, chunk), jnp.float32),
+            pltpu.VMEM((steps, CORES, chips, pairs, chunk), jnp.float32),
             pltpu.VMEM((steps, chips, pairs, chunk), jnp.float32),
             pltpu.VMEM((steps, chips, pairs, chunk), jnp.int16),
             pltpu.VMEM((steps, chips + 1, pairs, chunk), jnp.int16),
             pltpu.VMEM((2, steps, 1, chunk), jnp.float32),
             pltpu.VMEM((2, steps, 1, chunk), jnp.float32),
-            dma((blocks,)),
-            dma((blocks, cols)),
-            dma((blocks, cols)),
+            dma((blocks, CORES)),
+            dma((blocks, CORES, cols)),
+            dma((blocks, CORES, cols)),
             dma((SLOTS,)),
             dma((steps,)),
             dma((steps,)),
@@ -242,7 +281,7 @@
             collective_id=0, has_side_effects=True, vmem_limit_bytes=63 * 2**20
         ),
         name="ladder",
-    )(block_sizes, amplitudes.transpose(1, 0, 2), integrals)
+    )(block_sizes, amplitudes.reshape(CORES, pairs, blocks, span).transpose(2, 0, 1, 3), integrals)
     return result.transpose(1, 0, 2)
 
 

time: 114 us -> 109 us (0.956)
  Pallas kernels: 107 us -> 101 us
    pallas_call x1, Pallas kernels: 107 us -> 101 us  [body(): pl.pallas_call(functools.partial(kernel, chips, cols, steps, chunk), out_...]
where the time goes in v2:
time: 109 us; the launch traced here: 108 us
  Pallas kernels  101 us (93%)
  local copies, waits for them, and re-layouts  7.03 us (6%)
    pallas_call x1, Pallas kernels, body(): pl.pallas_call(functools.partial(kernel, chips, cols, steps, chunk), out_...  101 us
    transpose x1, local copies, waits for them, and re-layouts, body(): return result.transpose(1, 0, 2)  4.26 us
    unnamed x1, local copies, waits for them, and re-layouts  2.77 us

profile of v2, /device:TPU:0, one launch (start us, length us, event | category | flops | bytes accessed | tf_op | source)
XLA Modules:
  0.0 108.5 jit_solution(15906884050247944210)
XLA Ops:
  0.0 2.8 %copy.4 = bf16[64,4,2048]{2,0,1:T(8,128)(2,1)} copy(bf16[64,4,2048]{2,1,0:T(4,128)(2,1)} %param.3) | data formatting | bytes 2097152 | tf_op args[0]
  2.8 101.4 %ladder.1 = f32[4,32,4096]{2,1,0:T(8,128)} custom-call(s32[4]{0:T(128)} %sizes.1, bf16[4,2,32,2048]{3,2,1,0:T(8,128)(2,1)} %bitcast.5, bf16[4,2048,4096]{2,1,0:T(8,128)(2,1)} %integ.1), custom_call_target="tpu_custom_call" | custom-call | tf_op jit(solution)/shard_map/ladder/pallas_call | solution.py:250
  104.2 4.3 %copy.5 = f32[32,4,4096]{2,1,0:T(4,128)} copy(f32[32,4,4096]{2,0,1:T(8,128)} %bitcast.4) | data formatting | bytes 4194304 | tf_op jit(solution)/shard_map/transpose | solution.py:285
